TPU v7x, 32 devices: a whole 2x2x4 slice. The times are simulated.
32 devices in a mesh: rows: 4 (over z), cent: 8 (over y, x, core).
Axes of the slice: x: 2, y: 2, z: 4, core: 2. Of those that a mesh axis runs over, the one named last changes fastest.
Arguments:
- train_rows: float32 [16384, 64], P('rows'), may hold values from -6 to 6
- centre_index: int32 [16384], P('cent'), may hold values from 0 to 16383
- precond: bfloat16 [16384, 16384], P('cent', 'rows'), as said below
- coefficients: float32 [16384, 128], P(('rows', 'cent')), may hold values from -6 to 6
- residual: float32 [16384, 128], P(('rows', 'cent')), may hold values from -6 to 6
- direction: float32 [16384, 128], P(('rows', 'cent')), may hold values from -6 to 6
Outputs:
- coef_next: float32 [16384, 128], P(('rows', 'cent'))
- residual_next: float32 [16384, 128], P(('rows', 'cent'))
- direction_next: float32 [16384, 128], P(('rows', 'cent'))
Inputs may be any that keep to these rules, and one draw needn't show every extreme that they name: precond is zero below its diagonal.
All inputs are finite; a program needn't handle non-finite values.
Results may differ from a plain program's by a relative error of at most 0.0047.
Values may be sent and summed in bfloat16 or wider, within the bound.
A program may use at most 128 MiB of HBM per device.

v0:
```python
import math
import jax
import jax.numpy as jnp
from jax import lax
from jax.sharding import PartitionSpec as P

FEAT = 64
OUTS = 128
ridge_weight = 0.1


def kernel_tile(block_rows, centres):
    row_sq = jnp.sum(block_rows * block_rows, axis=1)
    cen_sq = jnp.sum(centres * centres, axis=1)
    cross = jnp.dot(
        block_rows, centres.T, precision=lax.Precision.HIGHEST, preferred_element_type=jnp.float32
    )
    distance = row_sq[:, None] + cen_sq[None, :] - 2.0 * cross
    return jnp.exp(-(2.0 / FEAT) * distance).astype(jnp.bfloat16)


def kernel_pass(local_rows, centres, coef_field, combine):
    count_rows = local_rows.shape[0]
    block_size = math.gcd(count_rows, 1024)
    block_count = count_rows // block_size
    groups = local_rows.reshape(block_count, block_size, FEAT)
    tiles = lax.map(lambda group_rows: kernel_tile(group_rows, centres), groups)
    fitted_part = jnp.einsum(
        "kbc,cd->kbd", tiles, coef_field, preferred_element_type=jnp.float32
    ).reshape(count_rows, OUTS)
    fitted = combine(fitted_part)
    fitted_groups = fitted.reshape(block_count, block_size, OUTS)
    grad_part = jnp.einsum("kbc,kbd->cd", tiles, fitted_groups, preferred_element_type=jnp.float32)
    return grad_part


def on_device(train_rows, centre_index, precond, coefficients, residual, direction):
    rows_here = train_rows.shape[0]
    start_row = lax.axis_index("rows") * rows_here
    offset = centre_index - start_row
    inside = ((offset >= 0) & (offset < rows_here)).astype(jnp.float32)
    picked = train_rows[jnp.clip(offset, 0, rows_here - 1)] * inside[:, None]
    centres = lax.psum(picked, "rows")
    dir_low = direction.astype(jnp.bfloat16)
    columns = precond
    partial_field = jnp.dot(
        columns,
        lax.all_gather(dir_low, "cent", axis=0, tiled=True),
        preferred_element_type=jnp.float32,
    )
    coef_field = lax.psum(partial_field, "rows").astype(jnp.bfloat16)

    def line_sum(part):
        return lax.psum(part, "cent").astype(jnp.bfloat16)

    grad_part = kernel_pass(train_rows, centres, coef_field, line_sum)
    grad = lax.psum(grad_part, "rows")
    grad_low = (grad * float(rows_here * lax.axis_size("rows")) ** (-0.5)).astype(jnp.bfloat16)
    columns = precond
    image = lax.psum_scatter(
        lax.dot_general(
            columns, grad_low, (((0,), (0,)), ((), ())), preferred_element_type=jnp.float32
        ),
        "cent",
        scatter_dimension=0,
        tiled=True,
    )
    image = image + ridge_weight * direction
    norm_old, curvature = lax.psum(
        (jnp.sum(residual * residual), jnp.sum(direction * image)), ("rows", "cent")
    )
    step_size = norm_old / curvature
    coef_next = coefficients + step_size * direction
    residual_next = residual - step_size * image
    norm_new = lax.psum(jnp.sum(residual_next * residual_next), ("rows", "cent"))
    direction_next = residual_next + norm_new / norm_old * direction
    return (coef_next, residual_next, direction_next)


def solution(mesh):
    placed = (
        P("rows", None),
        P("cent"),
        P("cent", "rows"),
        P(("rows", "cent"), None),
        P(("rows", "cent"), None),
        P(("rows", "cent"), None),
    )
    return jax.shard_map(
        on_device,
        mesh=mesh,
        in_specs=placed,
        out_specs=(P(("rows", "cent"), None), P(("rows", "cent"), None), P(("rows", "cent"), None)),
        check_vma=False,
    )
```

profile of v0, /device:TPU:0, one launch (start us, length us, event | category | flops | bytes accessed | tf_op | source)
XLA Modules:
  0.0 441.2 jit_solution(3471181950002680406)
XLA Ops:
  9.5 1.8 copy.9
  11.3 5.5 %gather_fusion = f32[2048,64]{1,0:T(8,128)S(1)} fusion(f32[4096,64]{1,0:T(8,128)S(1)} %copy.9, s32[2048]{0:T(1024)S(1)} %fusion.8), kind=kCustom, calls=%fused_computation | custom fusion | bytes 1056768 | tf_op jit(solution)/shard_map/gather | solution.py:42
  16.8 1.3 broadcast_multiply_fusion
  18.2 1.6 convert_element_type.21
  19.9 53.0 %all-reduce.6.cloned.1.call-done = f32[2048,64]{1,0:T(8,128)} async-done(((f32[2048,64]{1,0:T(8,128)}), f32[2048,64]{1,0:T(8,128)}) %all-reduce.6.cloned.1.call-update) | async-done | bytes 524304 | tf_op jit(solution)/shard_map/psum | solution.py:43
  72.9 1.6 multiply_reduce_fusion
  74.5 45.0 %while.12 = (s32[]{:T(128)}, bf16[4,1024,2048]{2,1,0:T(8,128)(2,1)}, f32[4,1024,64]{2,1,0:T(8,128)S(1)}, f32[2048]{0:T(1024)S(1)}, f32[2048,64]{1,0:T(8,128)}, /*index=5*/s32[]{:T(128)}) while((s32[]{:T(128)}, bf16[4,1024,2048]{2,1,0:T(8,128)(2,1)}, f32[4,1024,64]{2,1,0:T(8,128)S(1)}, f32[2048]{0:T(1024)S(1)}, f32[2048,64]{1,0:T(8,128)}, ...), condition=%wide.region_6.7_spmd, body=%wide.region_4.0_spmd.sunk | while | flops 1621228544 | bytes 6046793 | solution.py:27
  74.7 11.0 %bitcast_dynamic-update-slice_fusion.2 = bf16[4,1024,2048]{2,1,0:T(8,128)(2,1)} fusion(bf16[4,1024,2048]{2,1,0:T(8,128)(2,1)} %get-tuple-element.116, s32[]{:T(128)} %get-tuple-element.115, f32[2048,64]{1,0:T(8,128)} %get-tuple-element.125, f32[2048]{0:T(1024)S(1)} %get-tuple-element.124, f32[1024]{0:T(1024)S(1)} %fusion.23, ...), kind=kOutput, calls=%fused_computation.2.clone.1 | convolution fusion | flops 1621098496 | bytes 5780480 | tf_op jit(solution)/shard_map/while/body/eval_jaxpr/dot_general | solution.py:15
  85.9 11.1 %bitcast_dynamic-update-slice_fusion.2 = bf16[4,1024,2048]{2,1,0:T(8,128)(2,1)} fusion(bf16[4,1024,2048]{2,1,0:T(8,128)(2,1)} %get-tuple-element.116, s32[]{:T(128)} %get-tuple-element.115, f32[2048,64]{1,0:T(8,128)} %get-tuple-element.125, f32[2048]{0:T(1024)S(1)} %get-tuple-element.124, f32[1024]{0:T(1024)S(1)} %fusion.23, ...), kind=kOutput, calls=%fused_computation.2.clone.1 | convolution fusion | flops 1621098496 | bytes 5780480 | tf_op jit(solution)/shard_map/while/body/eval_jaxpr/dot_general | solution.py:15
  97.2 11.0 %bitcast_dynamic-update-slice_fusion.2 = bf16[4,1024,2048]{2,1,0:T(8,128)(2,1)} fusion(bf16[4,1024,2048]{2,1,0:T(8,128)(2,1)} %get-tuple-element.116, s32[]{:T(128)} %get-tuple-element.115, f32[2048,64]{1,0:T(8,128)} %get-tuple-element.125, f32[2048]{0:T(1024)S(1)} %get-tuple-element.124, f32[1024]{0:T(1024)S(1)} %fusion.23, ...), kind=kOutput, calls=%fused_computation.2.clone.1 | convolution fusion | flops 1621098496 | bytes 5780480 | tf_op jit(solution)/shard_map/while/body/eval_jaxpr/dot_general | solution.py:15
  108.4 11.1 %bitcast_dynamic-update-slice_fusion.2 = bf16[4,1024,2048]{2,1,0:T(8,128)(2,1)} fusion(bf16[4,1024,2048]{2,1,0:T(8,128)(2,1)} %get-tuple-element.116, s32[]{:T(128)} %get-tuple-element.115, f32[2048,64]{1,0:T(8,128)} %get-tuple-element.125, f32[2048]{0:T(1024)S(1)} %get-tuple-element.124, f32[1024]{0:T(1024)S(1)} %fusion.23, ...), kind=kOutput, calls=%fused_computation.2.clone.1 | convolution fusion | flops 1621098496 | bytes 5780480 | tf_op jit(solution)/shard_map/while/body/eval_jaxpr/dot_general | solution.py:15
  119.5 8.4 %fusion.10 = f32[2048,128]{1,0:T(8,128)S(1)} fusion(bf16[2048,4096]{1,0:T(8,128)(2,1)} %param.10, bf16[4096,128]{1,0:T(8,128)(2,1)} %all-gather.2.cloned.1.call-done), kind=kOutput, calls=%fused_computation.28 | convolution fusion | flops 2147483648 | bytes 18874368 | tf_op jit(solution)/shard_map/dot_general | solution.py:46
  127.9 41.5 %all-reduce.9 = bf16[2048,128]{1,0:T(8,128)(2,1)S(1)} all-reduce(f32[2048,128]{1,0:T(8,128)S(1)} %fusion.10), channel_id=1, replica_groups=mesh['rows'=4,'cent'=8] {'rows'}, use_global_device_ids=true, to_apply=%region_7.8 | all-reduce | flops 262144 | bytes 1572864 | tf_op jit(solution)/shard_map/psum | solution.py:51
  169.5 8.2 %fusion.4 = f32[4,1024,128]{2,1,0:T(8,128)S(1)} fusion(bf16[4,1024,2048]{2,1,0:T(8,128)(2,1)} %get-tuple-element.58, bf16[2048,128]{1,0:T(8,128)(2,1)S(1)} %all-reduce.9), kind=kOutput, calls=%fused_computation.12 | convolution fusion | flops 2147483648 | bytes 19398656 | tf_op jit(solution)/shard_map/kbc,cd->kbd/dot_general | solution.py:28
  177.6 56.6 %all-reduce.10 = bf16[4096,128]{1,0:T(8,128)(2,1)S(1)} all-reduce(f32[4096,128]{1,0:T(8,128)S(1)} %bitcast.34), channel_id=1, replica_groups=mesh['rows'=4,'cent'=8] {'cent'}, use_global_device_ids=true, to_apply=%region_8.9 | all-reduce | flops 524288 | bytes 3145728 | tf_op jit(solution)/shard_map/psum | solution.py:54
  234.2 9.2 %convolution_bitcast_fusion.1 = f32[2048,128]{1,0:T(8,128)} fusion(bf16[4,1024,2048]{2,1,0:T(8,128)(2,1)} %get-tuple-element.58, bf16[4,1024,128]{2,1,0:T(8,128)(2,1)S(1)} %bitcast.35), kind=kOutput, calls=%fused_computation.9 | convolution fusion | flops 2147483648 | bytes 18874368 | tf_op jit(solution)/shard_map/kbc,kbd->cd/dot_general | solution.py:33
  243.5 50.6 %all-reduce.8.cloned.1.call-done = f32[2048,128]{1,0:T(8,128)} async-done(((f32[2048,128]{1,0:T(8,128)}), f32[2048,128]{1,0:T(8,128)}) %all-reduce.8.cloned.1.call-update) | async-done | bytes 1048592 | tf_op jit(solution)/shard_map/psum | solution.py:57
  294.0 9.8 %convolution_bitcast_fusion = f32[4096,128]{0,1:T(8,128)} fusion(bf16[2048,4096]{1,0:T(8,128)(2,1)} %param.10, f32[2048,128]{1,0:T(8,128)} %all-reduce.8.cloned.1.call-done), kind=kOutput, calls=%fused_computation.8 | convolution fusion | flops 2148007936 | bytes 19922944 | tf_op jit(solution)/shard_map/dot_general | solution.py:61
  304.8 39.4 %reduce-scatter.2.cloned.1.call-done = f32[512,128]{0,1:T(8,128)} async-done(((f32[4096,128]{0,1:T(8,128)}), f32[512,128]{0,1:T(8,128)}) %reduce-scatter.2.cloned.1.call-update) | async-done | bytes 262160 | tf_op jit(solution)/shard_map/reduce_scatter | solution.py:60
  344.2 1.6 multiply_reduce_fusion.2
  346.0 39.6 %all-reduce = (f32[]{:T(128)}, f32[]{:T(128)}) all-reduce(f32[]{:T(128)} %multiply_reduce_fusion.3, f32[]{:T(128)} %multiply_reduce_fusion.2), channel_id=1, replica_groups=mesh['rows'=4,'cent'=8] {'rows','cent'}, use_global_device_ids=true, to_apply=%region_1.2 | all-reduce | flops 2 | bytes 16 | tf_op jit(solution)/shard_map/psum | solution.py:69
  386.9 1.6 multiply_reduce_fusion.1
  388.6 41.3 %psum.55 = f32[]{:T(128)} all-reduce(f32[]{:T(128)} %get-tuple-element.74), channel_id=1, replica_groups=mesh['rows'=4,'cent'=8] {'rows','cent'}, use_global_device_ids=true, to_apply=%region_14.15 | all-reduce | flops 1 | bytes 8 | tf_op jit(solution)/shard_map/psum | solution.py:75
  432.1 0.8 copy.17
  (29 shorter events, 5.3 us)
Async XLA Ops:
  8.0 64.9 %all-reduce.6.cloned.1.call-start = ((), (), s32[]{:S(2)}) async-start(), calls=%async_computation.1 | async-start | bytes 2097152 | tf_op jit(solution)/shard_map/psum | solution.py:43
  18.1 101.4 %all-gather.2.cloned.1.call-start = ((), (), s32[]{:S(2)}) async-start(), calls=%async_computation.2 | async-start | bytes 1179648 | tf_op jit(solution)/shard_map/all_gather | solution.py:48
  19.8 274.2 %all-reduce.8.cloned.1.call-start = ((), (), s32[]{:S(2)}) async-start(), calls=%async_computation.3 | async-start | bytes 2097152 | tf_op jit(solution)/shard_map/psum | solution.py:57
  243.4 60.5 %copy-start = (f32[512,128]{1,0:T(8,128)S(1)}, f32[512,128]{1,0:T(8,128)}, u32[]{:S(2)}) copy-start(f32[512,128]{1,0:T(8,128)} %param.13) | copy-start | bytes 786436
  243.4 60.7 %copy-start.1 = (f32[512,128]{1,0:T(8,128)S(1)}, f32[512,128]{1,0:T(8,128)}, u32[]{:S(2)}) copy-start(f32[512,128]{1,0:T(8,128)} %param.12) | copy-start | bytes 786436
  243.4 102.5 %copy-start.2 = (f32[512,128]{1,0:T(8,128)S(1)}, f32[512,128]{1,0:T(8,128)}, u32[]{:S(2)}) copy-start(f32[512,128]{1,0:T(8,128)} %param.11) | copy-start | bytes 786436
  243.4 100.8 %reduce-scatter.2.cloned.1.call-start = ((), (), s32[]{:S(2)}) async-start(), calls=%async_computation.4 | async-start | bytes 2359296 | tf_op jit(solution)/shard_map/reduce_scatter | solution.py:60
Sparse Core Ops, SparseCore 0:
  18.2 54.6 all-reduce.5
  243.5 50.4 all-reduce.7
Sparse Core Ops, SparseCore 1:
  21.1 25.9 all-gather.1
  304.0 40.2 reduce-scatter.1
where the time goes:
time: 442 us; the launch traced here: 441 us
  blocking collectives  179 us (40%)
  waiting for transfers between devices  143 us (32%)
  matrix products  79.7 us (18%)
  between operations  18.3 us (4%)
  other arithmetic  10.7 us (2%)
  local copies, waits for them, and re-layouts  10.2 us (2%)
    psum x1, blocking collectives, line_sum(): return lax.psum(part, 'cent').astype(jnp.bfloat16)  56.6 us
    psum x1, waiting for transfers between devices, on_device(): centres = lax.psum(picked, 'rows')  53 us
    psum x1, waiting for transfers between devices, on_device(): grad = lax.psum(grad_part, 'rows')  50.6 us
    dot_general x4, matrix products, kernel_tile(): jnp.dot(block_rows, centres.T, precision=lax.Precision.HIGHEST, preferred...  44.2 us
    psum x1, blocking collectives, on_device(): coef_field = lax.psum(partial_field, 'rows').astype(jnp.bfloat16)  41.5 us
    psum x1, blocking collectives, on_device(): lax.psum(jnp.sum(residual_next * residual_next), ('rows', 'cent'))  41.3 us
    psum x1, blocking collectives, on_device(): lax.psum((jnp.sum(residual * residual), jnp.sum(direction * image)), ('ro...  39.6 us
    reduce_scatter x1, waiting for transfers between devices, on_device(): lax.psum_scatter(lax.dot_general(columns, grad_low, (((0,), (0,)), ((), (...  39.4 us
  transfers between devices with their start and end apart: 4, of which 3 were waited for; matrix products, arithmetic and copies ran while one was open for 11% of the time, Pallas kernels for 0%

commit v1 on v0

--- a/solution.py
+++ b/solution.py
@@ -1,3 +1,4 @@
+import functools
 import math
 import jax
 import jax.numpy as jnp
@@ -7,6 +8,15 @@
 FEAT = 64
 OUTS = 128
 ridge_weight = 0.1
+
+
+def wrap_series(local_array, shard_axis, named_axis):
+    for i in (shard_axis, named_axis):
+        local_array = lax.psum(local_array, axis_name=i)
+    return local_array
+
+
+streams_write = functools.partial(wrap_series, shard_axis="rows", named_axis="cent")
 
 
 def kernel_tile(block_rows, centres):
@@ -66,9 +76,7 @@
         tiled=True,
     )
     image = image + ridge_weight * direction
-    norm_old, curvature = lax.psum(
-        (jnp.sum(residual * residual), jnp.sum(direction * image)), ("rows", "cent")
-    )
+    norm_old, curvature = streams_write((jnp.sum(residual * residual), jnp.sum(direction * image)))
     step_size = norm_old / curvature
     coef_next = coefficients + step_size * direction
     residual_next = residual - step_size * image

time: 442 us -> 424 us (0.959)
  blocking collectives: 179 us -> 160 us
    psum x1 -> x2, blocking collectives: 39.6 us -> 24.8 us  [wrap_series(): local_array = lax.psum(local_array, axis_name=i)]
  transfers between devices with their start and end apart: 4 -> 4, of which waited for: 3 -> 3; matrix products, arithmetic and copies ran while one was open for 11% -> 12% of each run, Pallas kernels for 0% -> 0%
where the time goes in v1:
time: 424 us; the launch traced here: 422 us
  blocking collectives  160 us (38%)
  waiting for transfers between devices  143 us (34%)
  matrix products  79.7 us (19%)
  between operations  18.3 us (4%)
  other arithmetic  10.7 us (3%)
  local copies, waits for them, and re-layouts  10.2 us (2%)
    psum x1, blocking collectives, line_sum(): return lax.psum(part, 'cent').astype(jnp.bfloat16)  56.6 us
    psum x1, waiting for transfers between devices, on_device(): centres = lax.psum(picked, 'rows')  53 us
    psum x1, waiting for transfers between devices, on_device(): grad = lax.psum(grad_part, 'rows')  50.6 us
    dot_general x4, matrix products, kernel_tile(): jnp.dot(block_rows, centres.T, precision=lax.Precision.HIGHEST, preferred...  44.2 us
    psum x1, blocking collectives, on_device(): coef_field = lax.psum(partial_field, 'rows').astype(jnp.bfloat16)  41.5 us
    reduce_scatter x1, waiting for transfers between devices, on_device(): lax.psum_scatter(lax.dot_general(columns, grad_low, (((0,), (0,)), ((), (...  39.4 us
    psum x1, blocking collectives, on_device(): lax.psum(jnp.sum(residual_next * residual_next), ('rows', 'cent'))  37 us
    psum x2, blocking collectives, wrap_series(): local_array = lax.psum(local_array, axis_name=i)  24.8 us
  transfers between devices with their start and end apart: 4, of which 3 were waited for; matrix products, arithmetic and copies ran while one was open for 12% of the time, Pallas kernels for 0%

profile of v1, /device:TPU:0, one launch (start us, length us, event | category | flops | bytes accessed | tf_op | source)
XLA Modules:
  0.0 422.1 jit_solution(12373093432765141799)
XLA Ops:
  9.5 1.8 copy.9
  11.3 5.5 %gather_fusion = f32[2048,64]{1,0:T(8,128)S(1)} fusion(f32[4096,64]{1,0:T(8,128)S(1)} %copy.9, s32[2048]{0:T(1024)S(1)} %fusion.8), kind=kCustom, calls=%fused_computation | custom fusion | bytes 1056768 | tf_op jit(solution)/shard_map/gather | solution.py:52
  16.8 1.3 broadcast_multiply_fusion
  18.2 1.6 convert_element_type.21
  19.9 53.0 %all-reduce.7.cloned.1.call-done = f32[2048,64]{1,0:T(8,128)} async-done(((f32[2048,64]{1,0:T(8,128)}), f32[2048,64]{1,0:T(8,128)}) %all-reduce.7.cloned.1.call-update) | async-done | bytes 524304 | tf_op jit(solution)/shard_map/psum | solution.py:53
  72.9 1.6 multiply_reduce_fusion
  74.5 45.0 %while.12 = (s32[]{:T(128)}, bf16[4,1024,2048]{2,1,0:T(8,128)(2,1)}, f32[4,1024,64]{2,1,0:T(8,128)S(1)}, f32[2048]{0:T(1024)S(1)}, f32[2048,64]{1,0:T(8,128)}, /*index=5*/s32[]{:T(128)}) while((s32[]{:T(128)}, bf16[4,1024,2048]{2,1,0:T(8,128)(2,1)}, f32[4,1024,64]{2,1,0:T(8,128)S(1)}, f32[2048]{0:T(1024)S(1)}, f32[2048,64]{1,0:T(8,128)}, ...), condition=%wide.region_7.8_spmd, body=%wide.region_5.7_spmd.sunk | while | flops 1621228544 | bytes 6046793 | solution.py:37
  74.7 11.0 %bitcast_dynamic-update-slice_fusion.2 = bf16[4,1024,2048]{2,1,0:T(8,128)(2,1)} fusion(bf16[4,1024,2048]{2,1,0:T(8,128)(2,1)} %get-tuple-element.118, s32[]{:T(128)} %get-tuple-element.117, f32[2048,64]{1,0:T(8,128)} %get-tuple-element.127, f32[2048]{0:T(1024)S(1)} %get-tuple-element.126, f32[1024]{0:T(1024)S(1)} %fusion.23, ...), kind=kOutput, calls=%fused_computation.2.clone.1 | convolution fusion | flops 1621098496 | bytes 5780480 | tf_op jit(solution)/shard_map/while/body/eval_jaxpr/dot_general | solution.py:25
  85.9 11.1 %bitcast_dynamic-update-slice_fusion.2 = bf16[4,1024,2048]{2,1,0:T(8,128)(2,1)} fusion(bf16[4,1024,2048]{2,1,0:T(8,128)(2,1)} %get-tuple-element.118, s32[]{:T(128)} %get-tuple-element.117, f32[2048,64]{1,0:T(8,128)} %get-tuple-element.127, f32[2048]{0:T(1024)S(1)} %get-tuple-element.126, f32[1024]{0:T(1024)S(1)} %fusion.23, ...), kind=kOutput, calls=%fused_computation.2.clone.1 | convolution fusion | flops 1621098496 | bytes 5780480 | tf_op jit(solution)/shard_map/while/body/eval_jaxpr/dot_general | solution.py:25
  97.2 11.0 %bitcast_dynamic-update-slice_fusion.2 = bf16[4,1024,2048]{2,1,0:T(8,128)(2,1)} fusion(bf16[4,1024,2048]{2,1,0:T(8,128)(2,1)} %get-tuple-element.118, s32[]{:T(128)} %get-tuple-element.117, f32[2048,64]{1,0:T(8,128)} %get-tuple-element.127, f32[2048]{0:T(1024)S(1)} %get-tuple-element.126, f32[1024]{0:T(1024)S(1)} %fusion.23, ...), kind=kOutput, calls=%fused_computation.2.clone.1 | convolution fusion | flops 1621098496 | bytes 5780480 | tf_op jit(solution)/shard_map/while/body/eval_jaxpr/dot_general | solution.py:25
  108.4 11.1 %bitcast_dynamic-update-slice_fusion.2 = bf16[4,1024,2048]{2,1,0:T(8,128)(2,1)} fusion(bf16[4,1024,2048]{2,1,0:T(8,128)(2,1)} %get-tuple-element.118, s32[]{:T(128)} %get-tuple-element.117, f32[2048,64]{1,0:T(8,128)} %get-tuple-element.127, f32[2048]{0:T(1024)S(1)} %get-tuple-element.126, f32[1024]{0:T(1024)S(1)} %fusion.23, ...), kind=kOutput, calls=%fused_computation.2.clone.1 | convolution fusion | flops 1621098496 | bytes 5780480 | tf_op jit(solution)/shard_map/while/body/eval_jaxpr/dot_general | solution.py:25
  119.5 8.4 %fusion.10 = f32[2048,128]{1,0:T(8,128)S(1)} fusion(bf16[2048,4096]{1,0:T(8,128)(2,1)} %param.10, bf16[4096,128]{1,0:T(8,128)(2,1)} %all-gather.2.cloned.1.call-done), kind=kOutput, calls=%fused_computation.28 | convolution fusion | flops 2147483648 | bytes 18874368 | tf_op jit(solution)/shard_map/dot_general | solution.py:56
  127.9 41.5 %all-reduce.10 = bf16[2048,128]{1,0:T(8,128)(2,1)S(1)} all-reduce(f32[2048,128]{1,0:T(8,128)S(1)} %fusion.10), channel_id=1, replica_groups=mesh['rows'=4,'cent'=8] {'rows'}, use_global_device_ids=true, to_apply=%region_8.9 | all-reduce | flops 262144 | bytes 1572864 | tf_op jit(solution)/shard_map/psum | solution.py:61
  169.5 8.2 %fusion.4 = f32[4,1024,128]{2,1,0:T(8,128)S(1)} fusion(bf16[4,1024,2048]{2,1,0:T(8,128)(2,1)} %get-tuple-element.58, bf16[2048,128]{1,0:T(8,128)(2,1)S(1)} %all-reduce.10), kind=kOutput, calls=%fused_computation.12 | convolution fusion | flops 2147483648 | bytes 19398656 | tf_op jit(solution)/shard_map/kbc,cd->kbd/dot_general | solution.py:38
  177.6 56.6 %all-reduce.11 = bf16[4096,128]{1,0:T(8,128)(2,1)S(1)} all-reduce(f32[4096,128]{1,0:T(8,128)S(1)} %bitcast.34), channel_id=1, replica_groups=mesh['rows'=4,'cent'=8] {'cent'}, use_global_device_ids=true, to_apply=%region_9.10 | all-reduce | flops 524288 | bytes 3145728 | tf_op jit(solution)/shard_map/psum | solution.py:64
  234.2 9.2 %convolution_bitcast_fusion.1 = f32[2048,128]{1,0:T(8,128)} fusion(bf16[4,1024,2048]{2,1,0:T(8,128)(2,1)} %get-tuple-element.58, bf16[4,1024,128]{2,1,0:T(8,128)(2,1)S(1)} %bitcast.35), kind=kOutput, calls=%fused_computation.9 | convolution fusion | flops 2147483648 | bytes 18874368 | tf_op jit(solution)/shard_map/kbc,kbd->cd/dot_general | solution.py:43
  243.5 50.6 %all-reduce.9.cloned.1.call-done = f32[2048,128]{1,0:T(8,128)} async-done(((f32[2048,128]{1,0:T(8,128)}), f32[2048,128]{1,0:T(8,128)}) %all-reduce.9.cloned.1.call-update) | async-done | bytes 1048592 | tf_op jit(solution)/shard_map/psum | solution.py:67
  294.0 9.8 %convolution_bitcast_fusion = f32[4096,128]{0,1:T(8,128)} fusion(bf16[2048,4096]{1,0:T(8,128)(2,1)} %param.10, f32[2048,128]{1,0:T(8,128)} %all-reduce.9.cloned.1.call-done), kind=kOutput, calls=%fused_computation.8 | convolution fusion | flops 2148007936 | bytes 19922944 | tf_op jit(solution)/shard_map/dot_general | solution.py:71
  304.8 39.4 %reduce-scatter.2.cloned.1.call-done = f32[512,128]{0,1:T(8,128)} async-done(((f32[4096,128]{0,1:T(8,128)}), f32[512,128]{0,1:T(8,128)}) %reduce-scatter.2.cloned.1.call-update) | async-done | bytes 262160 | tf_op jit(solution)/shard_map/reduce_scatter | solution.py:70
  344.2 1.6 multiply_reduce_fusion.2
  346.0 12.4 %all-reduce.1 = (f32[]{:T(128)}, f32[]{:T(128)}) all-reduce(f32[]{:T(128)} %multiply_reduce_fusion.3, f32[]{:T(128)} %multiply_reduce_fusion.2), channel_id=1, replica_groups=mesh['rows'=4,'cent'=8] {'rows'}, use_global_device_ids=true, to_apply=%region_1.2 | all-reduce | flops 2 | bytes 16 | tf_op jit(solution)/shard_map/psum | solution.py:15
  358.4 12.4 %all-reduce = (f32[]{:T(128)}, f32[]{:T(128)}) all-reduce(f32[]{:T(128)} %get-tuple-element.74, f32[]{:T(128)} %get-tuple-element.75), channel_id=1, replica_groups=mesh['rows'=4,'cent'=8] {'cent'}, use_global_device_ids=true, to_apply=%region_2.3 | all-reduce | flops 2 | bytes 16 | tf_op jit(solution)/shard_map/psum | solution.py:15
  372.1 1.6 multiply_reduce_fusion.1
  373.8 37.0 %psum.71 = f32[]{:T(128)} all-reduce(f32[]{:T(128)} %get-tuple-element.76), channel_id=1, replica_groups=mesh['rows'=4,'cent'=8] {'rows','cent'}, use_global_device_ids=true, to_apply=%region_16.17 | all-reduce | flops 1 | bytes 8 | tf_op jit(solution)/shard_map/psum | solution.py:83
  (30 shorter events, 6.1 us)
Async XLA Ops:
  8.0 64.9 %all-reduce.7.cloned.1.call-start = ((), (), s32[]{:S(2)}) async-start(), calls=%async_computation.1 | async-start | bytes 2097152 | tf_op jit(solution)/shard_map/psum | solution.py:53
  18.1 101.4 %all-gather.2.cloned.1.call-start = ((), (), s32[]{:S(2)}) async-start(), calls=%async_computation.2 | async-start | bytes 1179648 | tf_op jit(solution)/shard_map/all_gather | solution.py:58
  19.8 274.2 %all-reduce.9.cloned.1.call-start = ((), (), s32[]{:S(2)}) async-start(), calls=%async_computation.3 | async-start | bytes 2097152 | tf_op jit(solution)/shard_map/psum | solution.py:67
  243.4 60.5 %copy-start = (f32[512,128]{1,0:T(8,128)S(1)}, f32[512,128]{1,0:T(8,128)}, u32[]{:S(2)}) copy-start(f32[512,128]{1,0:T(8,128)} %param.13) | copy-start | bytes 786436
  243.4 60.7 %copy-start.1 = (f32[512,128]{1,0:T(8,128)S(1)}, f32[512,128]{1,0:T(8,128)}, u32[]{:S(2)}) copy-start(f32[512,128]{1,0:T(8,128)} %param.12) | copy-start | bytes 786436
  243.4 102.5 %copy-start.2 = (f32[512,128]{1,0:T(8,128)S(1)}, f32[512,128]{1,0:T(8,128)}, u32[]{:S(2)}) copy-start(f32[512,128]{1,0:T(8,128)} %param.11) | copy-start | bytes 786436
  243.4 100.8 %reduce-scatter.2.cloned.1.call-start = ((), (), s32[]{:S(2)}) async-start(), calls=%async_computation.4 | async-start | bytes 2359296 | tf_op jit(solution)/shard_map/reduce_scatter | solution.py:70
Sparse Core Ops, SparseCore 0:
  18.2 54.6 all-reduce.6
  243.5 50.4 all-reduce.8
Sparse Core Ops, SparseCore 1:
  21.1 25.9 all-gather.1
  304.0 40.2 reduce-scatter.1
